TPU v7x, 32 devices: a whole 2x2x4 slice. The times are simulated.
32 devices in a mesh: prow: 8 (over z, core), pcol: 4 (over y, x).
Axes of the slice: x: 2, y: 2, z: 4, core: 2. Of those that a mesh axis runs over, the one named last changes fastest.
Arguments:
- diag_block: float32 [256, 256], P('prow', 'pcol'), as said below
- panel: float32 [16384, 256], P('prow', 'pcol'), may hold values from -1.5 to 1.5
- slab: float32 [16384, 1024], P('prow', 'pcol'), may hold values from -6 to 6
Outputs:
- diag_factor: float32 [256, 256], P('prow', 'pcol')
- panel_factor: float32 [16384, 256], P('prow', 'pcol')
- slab_updated: float32 [16384, 1024], P('prow', 'pcol')
Inputs may be any that keep to these rules, and one draw needn't show every extreme that they name: diag_block is symmetric positive definite.
All inputs are finite; a program needn't handle non-finite values.
Results may differ from a plain program's by a relative error of at most 0.0003.
Values sent between devices are 32-bit elements; how exact they have to be, the bound alone decides.
A program may use at most 64 MiB of HBM per device.

v0:
```python
import jax
import jax.numpy as jnp
from jax import lax
from jax.sharding import PartitionSpec as P


def broadcast(block, axis, source):
    block = jnp.where(lax.axis_index(axis) == source, block, jnp.zeros_like(block))
    return lax.psum(block, axis)


def local(diag_block, panel, slab):
    row_count = lax.axis_size("prow")
    col_count = lax.axis_size("pcol")
    row_index = lax.axis_index("prow")
    col_index = lax.axis_index("pcol")
    diag_tile = lax.all_gather(diag_block, "pcol", axis=1, tiled=True)
    full_block = lax.all_gather(diag_tile, "prow", axis=0, tiled=True)
    diag_factor = jnp.linalg.cholesky(full_block)
    block_size = full_block.shape[0]
    col_width = panel.shape[1]
    local_rows = panel.shape[0]
    blocks_here = local_rows // block_size
    group = blocks_here * row_count // col_count
    full_rows = lax.all_gather(panel, "pcol", axis=1, tiled=True)
    inverse = jax.scipy.linalg.solve_triangular(
        diag_factor, jnp.eye(block_size, dtype=jnp.float32), lower=True
    )
    factor = jnp.dot(
        full_rows, inverse.T, precision=lax.Precision.HIGHEST, preferred_element_type=jnp.float32
    )
    diag_out = lax.dynamic_slice(
        diag_factor,
        (row_index * diag_block.shape[0], col_index * diag_block.shape[1]),
        (diag_block.shape[0], diag_block.shape[1]),
    )
    panel_out = lax.dynamic_slice_in_dim(factor, col_index * col_width, col_width, 1)
    target = col_index * group
    root_row = target % row_count
    local_block = target // row_count
    chosen = lax.dynamic_slice_in_dim(factor, local_block * block_size, block_size, 0)
    remote = broadcast(chosen, "prow", root_row)
    product = jnp.dot(
        factor, remote.T, precision=lax.Precision.HIGHEST, preferred_element_type=jnp.float32
    )
    position = jnp.arange(local_rows, dtype=jnp.int32)
    row_global = (
        position // block_size * row_count + row_index
    ) * block_size + position % block_size
    col_global = target * block_size + jnp.arange(block_size, dtype=jnp.int32)
    keep_mask = row_global[:, None] >= col_global[None, :]
    updated = jnp.where(keep_mask, slab - product, slab)
    return (diag_out, panel_out, updated)


def solution(mesh):
    placed = (P("prow", "pcol"), P("prow", "pcol"), P("prow", "pcol"))
    return jax.shard_map(
        local,
        mesh=mesh,
        in_specs=placed,
        out_specs=(P("prow", "pcol"), P("prow", "pcol"), P("prow", "pcol")),
        check_vma=False,
    )
```

profile of v0, /device:TPU:0, one launch (start us, length us, event | category | flops | bytes accessed | tf_op | source)
XLA Modules:
  0.0 166.8 jit_solution(1090098768620998737)
XLA Ops:
  7.2 0.7 all-gather.3.cloned.1.call-update
  8.0 9.9 %all-gather = f32[4,64,32]{1,2,0:T(8,128)S(1)} all-gather(f32[1,64,32]{1,2,0:T(8,128)} %bitcast.45), channel_id=1, replica_groups=mesh['prow'=8,'pcol'=4] {'pcol'}, dimensions={0}, use_global_device_ids=true | all-gather | bytes 40960 | tf_op jit(solution)/shard_map/all_gather | solution.py:17
  18.0 14.4 %all_gather.10 = f32[256,256]{1,0:T(8,128)S(1)} all-gather(f32[32,256]{1,0:T(8,128)S(1)} %bitcast.44), channel_id=1, replica_groups=mesh['prow'=8,'pcol'=4] {'prow'}, dimensions={0}, use_global_device_ids=true | all-gather | bytes 294912 | tf_op jit(solution)/shard_map/all_gather | solution.py:18
  32.6 11.7 %cholesky.50 = f32[128,128]{1,0:T(8,128)S(1)} custom-call(f32[128,128]{1,0:T(8,128)S(1)} %cholesky.118), custom_call_target="Cholesky" | custom-call | tf_op jit(solution)/shard_map/jit(cholesky)/cholesky | solution.py:19
  44.4 9.8 %custom-call.15 = f32[1,128,128]{1,2,0:T(8,128)S(1)} custom-call(f32[1,128,128]{2,1,0:T(8,128)S(1)} %get-tuple-element.26), custom_call_target="InvertDiagBlocksLowerTriangular" | custom-call | tf_op jit(solution)/shard_map/jit(cholesky)/cholesky | solution.py:19
  54.2 0.2 constant_dynamic-update-slice_fusion
  54.4 0.3 convolution_subtract_fusion.1
  54.7 11.7 %cholesky.105 = f32[128,128]{1,0:T(8,128)S(1)} custom-call(f32[128,128]{1,0:T(8,128)S(1)} %convolution_subtract_fusion.1), custom_call_target="Cholesky" | custom-call | tf_op jit(solution)/shard_map/jit(cholesky)/cholesky | solution.py:19
  66.4 0.6 compare_reduce_fusion
  68.5 4.1 %while.1 = (s32[]{:T(128)}, f32[256,256]{1,0:T(8,128)S(1)}, s32[2,2]{1,0:T(2,128)S(1)}, f32[2,128,128]{2,1,0:T(8,128)S(1)}, s32[]{:T(128)}) while((s32[]{:T(128)}, f32[256,256]{1,0:T(8,128)S(1)}, s32[2,2]{1,0:T(2,128)S(1)}, f32[2,128,128]{2,1,0:T(8,128)S(1)}, s32[]{:T(128)}) %tuple.28), condition=%wide.while_cond, body=%wide.while_body.sunk | while | flops 2 | bytes 131181 | solution.py:26
  68.7 0.6 fusion.34
  69.3 1.4 bitcast_dynamic-update-slice_fusion.2
  70.7 0.6 fusion.34
  71.3 1.4 bitcast_dynamic-update-slice_fusion.2
  72.7 19.7 %custom-call.16 = f32[2,128,128]{1,2,0:T(8,128)S(1)} custom-call(f32[2,128,128]{2,1,0:T(8,128)S(1)} %get-tuple-element.10), custom_call_target="InvertDiagBlocksLowerTriangular" | custom-call | tf_op jit(solution)/shard_map/jit(_solve_triangular)/triangular_solve | solution.py:26
  92.4 0.7 dynamic_slice.9
  93.1 0.3 fusion.6
  93.4 0.3 convolution_subtract_fusion
  93.7 0.3 fusion.9
  94.0 3.5 %fusion = f32[256,2048]{1,0:T(8,128)S(1)} fusion(f32[2048,256]{0,1:T(8,128)} %all-gather.3.cloned.1.call-done, f32[128,256]{1,0:T(8,128)S(1)} %fusion.9, f32[128,256]{1,0:T(8,128)S(1)} %fusion.6), kind=kOutput, calls=%fused_computation.6 | convolution fusion | flops 1610678272 | bytes 4456448 | tf_op jit(solution)/shard_map/dot_general | solution.py:29
  97.5 0.7 select_bitcast_fusion
  98.2 0.8 dynamic-slice_bitcast_fusion
  99.1 54.8 %all-reduce.3.cloned.1.call-done = f32[256,256]{0,1:T(8,128)} async-done(((f32[256,256]{0,1:T(8,128)}), f32[256,256]{0,1:T(8,128)}) %all-reduce.3.cloned.1.call-update) | async-done | bytes 262160 | tf_op jit(solution)/shard_map/psum | solution.py:9
  153.9 6.1 %subtract_select_fusion = f32[2048,256]{1,0:T(8,128)} fusion(f32[2048,256]{1,0:T(8,128)} %param.5, f32[256,2048]{1,0:T(8,128)S(1)} %fusion, f32[256,256]{0,1:T(8,128)} %all-reduce.3.cloned.1.call-done, s32[256]{0:T(256)S(1)} %iota_add_fusion, s32[2048]{0:T(1024)S(1)} %fusion.22), kind=kOutput, calls=%fused_computation.2 | convolution fusion | flops 1612185600 | bytes 6562816 | tf_op jit(solution)/shard_map/dot_general | solution.py:43
  (21 shorter events, 0.7 us)
Async XLA Ops:
  7.2 86.8 %all-gather.3.cloned.1.call-start = ((), (), s32[]{:S(2)}) async-start(), calls=%async_computation | async-start | bytes 2621440 | tf_op jit(solution)/shard_map/all_gather | solution.py:25
  7.9 146.0 %all-reduce.3.cloned.1.call-start = ((), (), s32[]{:S(2)}) async-start(), calls=%async_computation.1 | async-start | bytes 524288 | tf_op jit(solution)/shard_map/psum | solution.py:9
Sparse Core Ops, SparseCore 0:
  9.8 37.9 all-gather.2
  98.3 55.4 all-reduce.2
where the time goes:
time: 167 us
  waiting for transfers between devices  55.5 us (33%)
  other arithmetic  54.5 us (33%)
  blocking collectives  24.3 us (15%)
  between operations  15.5 us (9%)
  matrix products  10.9 us (7%)
  local copies, waits for them, and re-layouts  5.85 us (4%)
    psum x1, waiting for transfers between devices, broadcast(): return lax.psum(block, axis)  54.8 us
    another operation x6, other arithmetic, local(): diag_factor = jnp.linalg.cholesky(full_block)  34 us
    another operation x3, other arithmetic, local(): jax.scipy.linalg.solve_triangular(diag_factor, jnp.eye(block_size, dtype=...  19.7 us
    all_gather x1, blocking collectives, local(): full_block = lax.all_gather(diag_tile, 'prow', axis=0, tiled=True)  14.4 us
    all_gather x1, blocking collectives, local(): diag_tile = lax.all_gather(diag_block, 'pcol', axis=1, tiled=True)  9.88 us
    dot_general x1, matrix products, local(): jnp.dot(factor, remote.T, precision=lax.Precision.HIGHEST, preferred_elem...  6.11 us
    another operation x6, local copies, waits for them, and re-layouts  3.95 us
    dot_general x1, matrix products, local(): jnp.dot(full_rows, inverse.T, precision=lax.Precision.HIGHEST, preferred_...  3.47 us
  transfers between devices with their start and end apart: 2, of which 1 were waited for; matrix products, arithmetic and copies ran while one was open for 37% of the time, Pallas kernels for 0%

commit v1 on v0

v1 whole, which is shorter than its diff:
```python
import functools

import jax
import jax.numpy as jnp
from jax import lax
from jax.experimental import pallas as pl
from jax.experimental.pallas import tpu as pltpu
from jax.sharding import PartitionSpec as P

HI = lax.Precision.HIGHEST
F32 = jnp.float32
NB = 64


def small(groups, width):
    sub = lax.broadcasted_iota(jnp.int32, (8, 1), 0)
    for j in range(width):
        first, inner = divmod(j, 8)
        row = groups[first][inner : inner + 1, :]
        scale = lax.rsqrt(row[:, j : j + 1])
        row = row * scale
        for g in range(first, width // 8):
            column = groups[g][:, j : j + 1] * scale
            if g == first:
                column = jnp.where(sub > inner, column, 0.0)
                groups[g] = jnp.where(sub == inner, row, groups[g] - column * row)
            else:
                groups[g] = groups[g] - column * row
    return groups


def factor_block(work, upper, size, width, b):
    start, end = b * width, (b + 1) * width
    eye = (
        lax.broadcasted_iota(jnp.int32, (width, width), 0)
        == lax.broadcasted_iota(jnp.int32, (width, width), 1)
    ).astype(F32)
    both = jnp.concatenate([work[start:end, start:end], eye], axis=1)
    groups = small([both[8 * g : 8 * g + 8] for g in range(width // 8)], width)
    inverse = jnp.concatenate(groups, axis=0)[:, width:]
    rows = jnp.dot(inverse, work[start:end, :], precision=HI, preferred_element_type=F32)
    keep = (
        lax.broadcasted_iota(jnp.int32, (width, size), 1)
        >= lax.broadcasted_iota(jnp.int32, (width, size), 0) + start
    )
    left = jnp.where(keep, rows[:, :size], 0.0)
    upper[start:end, :] = left
    work[start:end, size:] = rows[:, size:]
    if end < size:
        column = left.T[end:, :]
        work[end:, :] = work[end:, :] - jnp.dot(
            column,
            jnp.concatenate([left, rows[:, size:]], axis=1),
            precision=HI,
            preferred_element_type=F32,
        )


def gather_kernel(
    rows, cols, group,
    diag, panel,
    gathered, lower, inverse, strip,
    tiles, work, upper, strip_in, strip_all,
    tile_send, tile_recv, wide_send, wide_recv, own_sem,
    panel_send, panel_recv, strip_send, strip_recv, ex_send, ex_recv, copy_sem,
):
    row, col = lax.axis_index("prow"), lax.axis_index("pcol")
    size = upper.shape[0]

    def down(d):
        return {"prow": lax.rem(row + d, rows)}

    def across(d):
        return {"pcol": lax.rem(col + d, cols)}

    def remote(src, dst, send, recv, to):
        return pltpu.make_async_remote_copy(
            src_ref=src, dst_ref=dst, send_sem=send, recv_sem=recv,
            device_id=to, device_id_type=pl.DeviceIdType.MESH,
        )

    barrier = pltpu.get_barrier_semaphore()
    for d in range(1, rows):
        pl.semaphore_signal(barrier, inc=1, device_id=down(d), device_id_type=pl.DeviceIdType.MESH)
    for d in range(1, cols):
        pl.semaphore_signal(barrier, inc=1, device_id=across(d), device_id_type=pl.DeviceIdType.MESH)
    own_tile = pltpu.make_async_copy(diag, tiles.at[col, row], own_sem.at[0])
    own_tile.start()
    own_panel = pltpu.make_async_copy(panel, gathered.at[col], own_sem.at[1])
    own_panel.start()
    pl.semaphore_wait(barrier, rows + cols - 2)

    tile_copies = [
        remote(diag, tiles.at[col, row], tile_send.at[d], tile_recv.at[d], down(d))
        for d in range(1, rows)
    ]
    for copy in tile_copies:
        copy.start()
    own_tile.wait()
    for copy in tile_copies:
        copy.wait()
    wide = [
        remote(tiles.at[col], tiles.at[col], wide_send.at[d], wide_recv.at[d], across(d))
        for d in range(1, cols)
    ]
    for copy in wide:
        copy.start()

    def strip_block(c):
        return panel.at[pl.ds((c * group // rows) * size, size)]

    def strip_copy(c, d):
        return remote(
            strip_block(c), strip_in.at[c], strip_send.at[c, d], strip_recv.at[c], down(d)
        )

    for c in range(cols):
        root = (c * group) % rows

        @pl.when(row == root)
        def _():
            pltpu.make_async_copy(strip_block(c), strip_in.at[c], copy_sem.at[c]).start()
            for d in range(1, rows):
                strip_copy(c, d).start()

    for copy in wide:
        copy.wait()
    panels = [
        remote(panel, gathered.at[col], panel_send.at[d], panel_recv.at[d], across(d))
        for d in range(1, cols)
    ]
    for copy in panels:
        copy.start()

    for c in range(cols):
        for r in range(rows):
            high, low = tiles.shape[2], tiles.shape[3]
            work[r * high : (r + 1) * high, c * low : (c + 1) * low] = tiles[c, r]
    work[:, size:] = (
        lax.broadcasted_iota(jnp.int32, (size, size), 0)
        == lax.broadcasted_iota(jnp.int32, (size, size), 1)
    ).astype(F32)

    blocks = size // NB
    exchange = [
        remote(
            strip_in.at[lax.rem(col + d, cols)], strip_all.at[col],
            ex_send.at[d], ex_recv.at[d], across(d),
        )
        for d in range(1, cols)
    ]
    own_strip = pltpu.make_async_copy(strip_in.at[col], strip_all.at[col], own_sem.at[2])
    for b in range(blocks):
        factor_block(work, upper, size, NB, b)
        if b == blocks - 2:
            for c in range(cols):
                root = (c * group) % rows

                @pl.when(row == root)
                def _():
                    pltpu.make_async_copy(strip_block(c), strip_in.at[c], copy_sem.at[c]).wait()
                    for d in range(1, rows):
                        strip_copy(c, d).wait_send()

                @pl.when(row != root)
                def _():
                    strip_copy(c, 1).wait_recv()

            own_strip.start()
            for copy in exchange:
                copy.start()
    lower[...] = upper[...].T
    inverse[...] = work[:, size:]
    own_strip.wait()
    for copy in exchange:
        copy.wait()
    full = jnp.concatenate([strip_all[c] for c in range(cols)], axis=1)
    strip[...] = lax.dot_general(
        full, work[:, size:], (((1,), (1,)), ((), ())), precision=HI, preferred_element_type=F32
    )
    own_panel.wait()
    for copy in panels:
        copy.wait()


def split(x):
    high = x.astype(jnp.bfloat16)
    return high, (x - high.astype(F32)).astype(jnp.bfloat16)


def dot_t(a, b):
    dims = (((1,), (1,)), ((), ()))
    (ah, al), (bh, bl) = a, b
    dot = functools.partial(lax.dot_general, dimension_numbers=dims, preferred_element_type=F32)
    return dot(ah, bh) + (dot(ah, bl) + dot(al, bh))


def update_kernel(rows, cols, group, gathered, inverse, strip, slab, panel_out, slab_out):
    row, col = lax.axis_index("prow"), lax.axis_index("pcol")
    block, size = pl.program_id(0), slab.shape[0]
    low = gathered.shape[2]
    full = jnp.concatenate([gathered[c] for c in range(cols)], axis=1)
    factor = dot_t(split(full), split(inverse[...]))
    for c in range(cols):

        @pl.when(col == c)
        def _():
            panel_out[...] = factor[:, c * low : (c + 1) * low]

    product = dot_t(split(factor), split(strip[...]))
    shift = (block * rows + row - col * group) * size
    keep = (
        lax.broadcasted_iota(jnp.int32, slab.shape, 0) + shift
        >= lax.broadcasted_iota(jnp.int32, slab.shape, 1)
    )
    slab_out[...] = jnp.where(keep, slab[...] - product, slab[...])


def local(rows, cols, diag_block, panel, slab):
    high, low = diag_block.shape
    size = high * rows
    local_rows, width = panel.shape
    blocks = local_rows // size
    group = blocks * rows // cols
    any_spec = pl.BlockSpec(memory_space=pl.ANY)
    vmem = pl.BlockSpec(memory_space=pltpu.VMEM)
    dma = pltpu.SemaphoreType.DMA
    square = jax.ShapeDtypeStruct((size, size), F32)
    gathered, lower, inverse, strip = pl.pallas_call(
        functools.partial(gather_kernel, rows, cols, group),
        out_shape=[jax.ShapeDtypeStruct((cols, local_rows, width), F32), square, square, square],
        in_specs=[vmem, any_spec],
        out_specs=[any_spec, vmem, vmem, vmem],
        scratch_shapes=[
            pltpu.VMEM((cols, rows, high, low), F32),
            pltpu.VMEM((size, 2 * size), F32),
            pltpu.VMEM((size, size), F32),
            pltpu.VMEM((cols, size, width), F32),
            pltpu.VMEM((cols, size, width), F32),
            dma((rows,)), dma((rows,)), dma((cols,)), dma((cols,)), dma((3,)),
            dma((cols,)), dma((cols,)), dma((cols, rows)), dma((cols,)),
            dma((cols,)), dma((cols,)), dma((cols,)),
        ],
        compiler_params=pltpu.CompilerParams(collective_id=0, has_side_effects=True),
        name="gather_factor",
    )(diag_block, panel)
    panel_out, slab_out = pl.pallas_call(
        functools.partial(update_kernel, rows, cols, group),
        grid=(blocks,),
        out_shape=[
            jax.ShapeDtypeStruct(panel.shape, F32),
            jax.ShapeDtypeStruct(slab.shape, F32),
        ],
        in_specs=[
            pl.BlockSpec((cols, size, width), lambda i: (0, i, 0)),
            pl.BlockSpec((size, size), lambda i: (0, 0)),
            pl.BlockSpec((size, size), lambda i: (0, 0)),
            pl.BlockSpec((size, slab.shape[1]), lambda i: (i, 0)),
        ],
        out_specs=[
            pl.BlockSpec((size, width), lambda i: (i, 0)),
            pl.BlockSpec((size, slab.shape[1]), lambda i: (i, 0)),
        ],
        name="update",
    )(gathered, inverse, strip, slab)
    diag_out = lax.dynamic_slice(
        lower, (lax.axis_index("prow") * high, lax.axis_index("pcol") * low), (high, low)
    )
    return diag_out, panel_out, slab_out


def solution(mesh):
    spec = P("prow", "pcol")
    return jax.shard_map(
        functools.partial(local, mesh.shape["prow"], mesh.shape["pcol"]),
        mesh=mesh,
        in_specs=(spec, spec, spec),
        out_specs=(spec, spec, spec),
        check_vma=False,
    )
```

time: 167 us -> 89.4 us (0.54)
  Pallas kernels: 0 us -> 82.1 us
  waiting for transfers between devices: 55.5 us -> 0 us
  other arithmetic: 54.5 us -> 0 us
  blocking collectives: 24.3 us -> 0 us
  between operations: 15.5 us -> 0.65 us
  matrix products: 10.9 us -> 0 us
    pallas_call x0 -> x2, Pallas kernels: none -> 82.1 us  [the longest x1 72.4 us: local(): pl.pallas_call(functools.partial(gather_kernel, rows, cols, group), out_s...]
    psum x1 -> x0, waiting for transfers between devices: 54.8 us -> none  [broadcast(): return lax.psum(block, axis)]
    another operation x9 -> x0, other arithmetic: 53.7 us -> none  [the longest x6 34 us: local(): diag_factor = jnp.linalg.cholesky(full_block)]
    all_gather x2 -> x0, blocking collectives: 24.3 us -> none  [the longest x1 14.4 us: local(): full_block = lax.all_gather(diag_tile, 'prow', axis=0, tiled=True)]
    dot_general x2 -> x0, matrix products: 9.57 us -> none  [the longest x1 6.11 us: local(): jnp.dot(factor, remote.T, precision=lax.Precision.HIGHEST, preferred_elem...]
    unnamed x1 -> x2, local copies, waits for them, and re-layouts: 0.1 us -> 4.69 us
    another operation x9 -> x0, local copies, waits for them, and re-layouts: 4.05 us -> none
  transfers between devices with their start and end apart: 2 -> 0, of which waited for: 1 -> 0; matrix products, arithmetic and copies ran while one was open for 37% -> 0% of each run, Pallas kernels for 0% -> 0%
where the time goes in v1:
time: 89.4 us; the launch traced here: 88.9 us
  Pallas kernels  82.1 us (92%)
  local copies, waits for them, and re-layouts  6.09 us (7%)
    pallas_call x1, Pallas kernels, local(): pl.pallas_call(functools.partial(gather_kernel, rows, cols, group), out_s...  72.4 us
    pallas_call x1, Pallas kernels, local(): pl.pallas_call(functools.partial(update_kernel, rows, cols, group), grid=...  9.77 us
    unnamed x2, local copies, waits for them, and re-layouts  4.69 us

profile of v1, /device:TPU:0, one launch (start us, length us, event | category | flops | bytes accessed | tf_op | source)
XLA Modules:
  0.0 88.9 jit_solution(7337493706271753711)
XLA Ops:
  0.6 2.4 %copy.6.panel = f32[2048,64]{1,0:T(8,128)} copy(f32[2048,64]{0,1:T(8,128)} %param.4) | data formatting | bytes 1048576 | tf_op args[1]
  3.0 72.4 %gather_factor.1 = (f32[4,2048,64]{2,1,0:T(8,128)}, f32[256,256]{1,0:T(8,128)}, f32[256,256]{1,0:T(8,128)}, f32[256,256]{1,0:T(8,128)}) custom-call(f32[32,64]{1,0:T(8,128)} %diag.1, f32[2048,64]{1,0:T(8,128)} %copy.6.panel), custom_call_target="tpu_custom_call" | custom-call | tf_op jit(solution)/shard_map/gather_factor/pallas_call | solution.py:229
  75.4 1.4 %dynamic_slice.3 = f32[32,64]{1,0:T(8,128)} dynamic-slice(f32[256,256]{1,0:T(8,128)} %get-tuple-element.9, s32[]{:T(128)S(6)} %select_n.6, s32[]{:T(128)S(6)} %select_n.7), dynamic_slice_sizes={32,64} | dynamic-slice | bytes 16388 | tf_op jit(solution)/shard_map/dynamic_slice | solution.py:266
  76.8 9.8 %update.1 = (f32[2048,64]{1,0:T(8,128)}, f32[2048,256]{1,0:T(8,128)}) custom-call(f32[4,2048,64]{2,1,0:T(8,128)} %get-tuple-element.10.gathered, f32[256,256]{1,0:T(8,128)} %get-tuple-element.11.inverse, f32[256,256]{1,0:T(8,128)} %get-tuple-element.12.strip, f32[2048,256]{1,0:T(8,128)} %slab.1), custom_call_target="tpu_custom_call" | custom-call | tf_op jit(solution)/shard_map/update/pallas_call | solution.py:247
  86.6 2.3 %copy.7 = f32[2048,64]{0,1:T(8,128)} copy(f32[2048,64]{1,0:T(8,128)} %get-tuple-element.16) | data formatting | bytes 1048576

commit v2 on v1

--- a/solution.py
+++ b/solution.py
@@ -107,7 +107,7 @@
         copy.start()
 
     def strip_block(c):
-        return panel.at[pl.ds((c * group // rows) * size, size)]
+        return panel.at[:, pl.ds((c * group // rows) * size, size)]
 
     def strip_copy(c, d):
         return remote(
@@ -174,9 +174,11 @@
     own_strip.wait()
     for copy in exchange:
         copy.wait()
-    full = jnp.concatenate([strip_all[c] for c in range(cols)], axis=1)
-    strip[...] = lax.dot_general(
-        full, work[:, size:], (((1,), (1,)), ((), ())), precision=HI, preferred_element_type=F32
+    strip[...] = jnp.dot(
+        work[:, size:],
+        strip_all[...].reshape(size, size),
+        precision=HI,
+        preferred_element_type=F32,
     )
     own_panel.wait()
     for copy in panels:
@@ -188,26 +190,33 @@
     return high, (x - high.astype(F32)).astype(jnp.bfloat16)
 
 
-def dot_t(a, b):
-    dims = (((1,), (1,)), ((), ()))
+def dot_split(a, b):
     (ah, al), (bh, bl) = a, b
-    dot = functools.partial(lax.dot_general, dimension_numbers=dims, preferred_element_type=F32)
+    dot = functools.partial(jnp.dot, preferred_element_type=F32)
     return dot(ah, bh) + (dot(ah, bl) + dot(al, bh))
 
 
-def update_kernel(rows, cols, group, gathered, inverse, strip, slab, panel_out, slab_out):
+def update_kernel(
+    rows, cols, group, gathered, inverse, strip, lower, slab, diag_out, panel_out, slab_out
+):
     row, col = lax.axis_index("prow"), lax.axis_index("pcol")
     block, size = pl.program_id(0), slab.shape[0]
-    low = gathered.shape[2]
-    full = jnp.concatenate([gathered[c] for c in range(cols)], axis=1)
-    factor = dot_t(split(full), split(inverse[...]))
+    high, low = diag_out.shape
+
+    full = gathered[...].reshape(size, size)
+    factor = dot_split(split(inverse[...]), split(full))
     for c in range(cols):
 
         @pl.when(col == c)
         def _():
-            panel_out[...] = factor[:, c * low : (c + 1) * low]
-
-    product = dot_t(split(factor), split(strip[...]))
+            panel_out[...] = factor[c * low : (c + 1) * low, :]
+
+            @pl.when(block == 0)
+            def _():
+                start = pl.multiple_of(row * high, high)
+                diag_out[...] = lower[pl.ds(start, high), c * low : (c + 1) * low]
+
+    product = dot_split(split(factor.T), split(strip[...]))
     shift = (block * rows + row - col * group) * size
     keep = (
         lax.broadcasted_iota(jnp.int32, slab.shape, 0) + shift
@@ -228,45 +237,46 @@
     square = jax.ShapeDtypeStruct((size, size), F32)
     gathered, lower, inverse, strip = pl.pallas_call(
         functools.partial(gather_kernel, rows, cols, group),
-        out_shape=[jax.ShapeDtypeStruct((cols, local_rows, width), F32), square, square, square],
+        out_shape=[jax.ShapeDtypeStruct((cols, width, local_rows), F32), square, square, square],
         in_specs=[vmem, any_spec],
         out_specs=[any_spec, vmem, vmem, vmem],
         scratch_shapes=[
             pltpu.VMEM((cols, rows, high, low), F32),
             pltpu.VMEM((size, 2 * size), F32),
             pltpu.VMEM((size, size), F32),
-            pltpu.VMEM((cols, size, width), F32),
-            pltpu.VMEM((cols, size, width), F32),
+            pltpu.VMEM((cols, width, size), F32),
+            pltpu.VMEM((cols, width, size), F32),
             dma((rows,)), dma((rows,)), dma((cols,)), dma((cols,)), dma((3,)),
             dma((cols,)), dma((cols,)), dma((cols, rows)), dma((cols,)),
             dma((cols,)), dma((cols,)), dma((cols,)),
         ],
         compiler_params=pltpu.CompilerParams(collective_id=0, has_side_effects=True),
         name="gather_factor",
-    )(diag_block, panel)
-    panel_out, slab_out = pl.pallas_call(
+    )(diag_block, panel.T)
+    whole = pl.BlockSpec((size, size), lambda i: (0, 0))
+    diag_out, panel_out, slab_out = pl.pallas_call(
         functools.partial(update_kernel, rows, cols, group),
         grid=(blocks,),
         out_shape=[
-            jax.ShapeDtypeStruct(panel.shape, F32),
+            jax.ShapeDtypeStruct(diag_block.shape, F32),
+            jax.ShapeDtypeStruct((width, local_rows), F32),
             jax.ShapeDtypeStruct(slab.shape, F32),
         ],
         in_specs=[
-            pl.BlockSpec((cols, size, width), lambda i: (0, i, 0)),
-            pl.BlockSpec((size, size), lambda i: (0, 0)),
-            pl.BlockSpec((size, size), lambda i: (0, 0)),
+            pl.BlockSpec((cols, width, size), lambda i: (0, 0, i)),
+            whole,
+            whole,
+            whole,
             pl.BlockSpec((size, slab.shape[1]), lambda i: (i, 0)),
         ],
         out_specs=[
-            pl.BlockSpec((size, width), lambda i: (i, 0)),
+            pl.BlockSpec((high, low), lambda i: (0, 0)),
+            pl.BlockSpec((width, size), lambda i: (0, i)),
             pl.BlockSpec((size, slab.shape[1]), lambda i: (i, 0)),
         ],
         name="update",
-    )(gathered, inverse, strip, slab)
-    diag_out = lax.dynamic_slice(
-        lower, (lax.axis_index("prow") * high, lax.axis_index("pcol") * low), (high, low)
-    )
-    return diag_out, panel_out, slab_out
+    )(gathered, inverse, strip, lower, slab)
+    return diag_out, panel_out.T, slab_out
 
 
 def solution(mesh):

time: 89.4 us -> 57.4 us (0.64)
  Pallas kernels: 82.1 us -> 56.5 us
  local copies, waits for them, and re-layouts: 6.09 us -> 0 us
    pallas_call x1, Pallas kernels: 72.4 us -> 47.1 us  [local(): pl.pallas_call(functools.partial(gather_kernel, rows, cols, group), out_s...]
    unnamed x2 -> x0, local copies, waits for them, and re-layouts: 4.69 us -> none
    dynamic_slice x1 -> x0, local copies, waits for them, and re-layouts: 1.41 us -> none  [local(): lax.dynamic_slice(lower, (lax.axis_index('prow') * high, lax.axis_index('...]
where the time goes in v2:
time: 57.4 us; the launch traced here: 57.1 us
  Pallas kernels  56.5 us (98%)
  between operations  0.64 us (1%)
    pallas_call x1, Pallas kernels, local(): pl.pallas_call(functools.partial(gather_kernel, rows, cols, group), out_s...  47.1 us
    pallas_call x1, Pallas kernels, local(): pl.pallas_call(functools.partial(update_kernel, rows, cols, group), grid=...  9.36 us

profile of v2, /device:TPU:0, one launch (start us, length us, event | category | flops | bytes accessed | tf_op | source)
XLA Modules:
  0.0 57.1 jit_solution(13631901835128698828)
XLA Ops:
  0.6 47.1 %gather_factor.1 = (f32[4,64,2048]{2,1,0:T(8,128)}, f32[256,256]{1,0:T(8,128)}, f32[256,256]{1,0:T(8,128)}, f32[256,256]{1,0:T(8,128)}) custom-call(f32[32,64]{1,0:T(8,128)} %diag.1, f32[64,2048]{1,0:T(8,128)} %bitcast.2), custom_call_target="tpu_custom_call" | custom-call | tf_op jit(solution)/shard_map/gather_factor/pallas_call | solution.py:238
  47.7 9.4 %update.1 = (f32[32,64]{1,0:T(8,128)}, f32[64,2048]{1,0:T(8,128)}, f32[2048,256]{1,0:T(8,128)}) custom-call(f32[4,64,2048]{2,1,0:T(8,128)} %get-tuple-element.10.gathered, f32[256,256]{1,0:T(8,128)} %get-tuple-element.11.inverse, f32[256,256]{1,0:T(8,128)} %get-tuple-element.12.strip, f32[256,256]{1,0:T(8,128)} %get-tuple-element.13.lower, f32[2048,256]{1,0:T(8,128)} %slab.1), custom_call_target="tpu_custom_call" | custom-call | tf_op jit(solution)/shard_map/update/pallas_call | solution.py:257

commit v3 on v2

--- a/solution.py
+++ b/solution.py
@@ -10,22 +10,49 @@
 HI = lax.Precision.HIGHEST
 F32 = jnp.float32
 NB = 64
+TILE = 2
 
 
 def small(groups, width):
-    sub = lax.broadcasted_iota(jnp.int32, (8, 1), 0)
-    for j in range(width):
-        first, inner = divmod(j, 8)
-        row = groups[first][inner : inner + 1, :]
-        scale = lax.rsqrt(row[:, j : j + 1])
-        row = row * scale
-        for g in range(first, width // 8):
-            column = groups[g][:, j : j + 1] * scale
-            if g == first:
-                column = jnp.where(sub > inner, column, 0.0)
-                groups[g] = jnp.where(sub == inner, row, groups[g] - column * row)
-            else:
-                groups[g] = groups[g] - column * row
+    lanes = 2 * width
+    sub = lax.broadcasted_iota(jnp.int32, (8, lanes), 0)
+    eight = range(8)
+
+    def spread(x):
+        return jnp.broadcast_to(x, (8, lanes))
+
+    for g0 in range(width // 8):
+        base, first = groups[g0], 8 * g0
+        columns = [spread(base[:, first + k : first + k + 1]) for k in eight]
+        d = {(m, k): spread(columns[k][m : m + 1, :]) for k in eight for m in range(k, 8)}
+        rows = [spread(base[k : k + 1, :]) for k in eight]
+        scales = []
+        for k in eight:
+            scale = lax.rsqrt(d[k, k])
+            scales.append(scale)
+            for m in range(k + 1, 8):
+                d[m, k] = d[m, k] * scale
+            for m in range(k + 1, 8):
+                for q in range(k + 1, m + 1):
+                    d[m, q] = d[m, q] - d[m, k] * d[q, k]
+            rows[k] = rows[k] * scale
+            for m in range(k + 1, 8):
+                rows[m] = rows[m] - d[m, k] * rows[k]
+        back = [None] * 8
+        for k in reversed(eight):
+            total = rows[k]
+            for m in range(k + 1, 8):
+                total = total - d[m, k] * back[m]
+            back[k] = total * scales[k]
+        solved = rows[0]
+        for k in range(1, 8):
+            solved = jnp.where(sub == k, rows[k], solved)
+        groups[g0] = solved
+        for g in range(g0 + 1, width // 8):
+            terms = [spread(groups[g][:, first + k : first + k + 1]) * back[k] for k in eight]
+            while len(terms) > 1:
+                terms = [x + y for x, y in zip(terms[::2], terms[1::2])]
+            groups[g] = groups[g] - terms[0]
     return groups
 
 
@@ -66,6 +93,7 @@
 ):
     row, col = lax.axis_index("prow"), lax.axis_index("pcol")
     size = upper.shape[0]
+    piece = panel.shape[1] // 4
 
     def down(d):
         return {"prow": lax.rem(row + d, rows)}
@@ -96,6 +124,75 @@
     ]
     for copy in tile_copies:
         copy.start()
+
+    def part(i):
+        return pl.ds(i * piece, piece)
+
+    def piece_copy(i, d, to):
+        return remote(
+            panel.at[:, part(i)], gathered.at[col, :, part(i)],
+            panel_send.at[d, i], panel_recv.at[d, i], to,
+        )
+
+    relay = cols == 4
+    forwards = []
+    if relay:
+        side, other = col + 1 - 2 * lax.rem(col, 2), lax.rem(col + 2, 4)
+        to_side, to_other = {"pcol": side}, {"pcol": other}
+        early = [piece_copy(0, 0, to_side), piece_copy(2, 1, to_other)]
+        late = []
+        for i in range(1, 4):
+            late += [piece_copy(i, 0, to_side), piece_copy((i + 2) % 4, 1, to_other)]
+        lower_half, upper_half = pl.ds(0, 2 * piece), pl.ds(2 * piece, 2 * piece)
+        for slot, (source, half, to) in enumerate(
+            [(side, lower_half, to_other), (other, upper_half, to_side)]
+        ):
+            view = gathered.at[source, :, half]
+            forwards.append(remote(view, view, panel_send.at[2, slot], panel_recv.at[2, slot], to))
+    else:
+        early = []
+        late = [piece_copy(i, d, across(d)) for d in range(1, cols) for i in range(4)]
+    for copy in early:
+        copy.start()
+
+    def strip_block(c):
+        return panel.at[:, pl.ds((c * group // rows) * size, size)]
+
+    def strip_sends(c, src):
+        root = (c * group) % rows
+        place, origin, last = row // 2, root // 2, rows // 2 - 1
+        spine = lax.rem(row, 2) == root % 2
+        steps = [
+            (spine & (place >= origin) & (place < last), 2),
+            (spine & (place <= origin) & (place > 0), -2),
+            (spine, 1 - 2 * (root % 2)),
+        ]
+        return [
+            (
+                cond,
+                remote(
+                    src, strip_in.at[c], strip_send.at[c, i], strip_recv.at[c],
+                    {"prow": lax.rem(row + step + rows, rows)},
+                ),
+            )
+            for i, (cond, step) in enumerate(steps)
+        ]
+
+    def strip_start(c, src):
+        for cond, copy in strip_sends(c, src):
+            pl.when(cond)(copy.start)
+
+    def strip_own(c):
+        return pltpu.make_async_copy(strip_block(c), strip_in.at[c], copy_sem.at[c])
+
+    for c in range(cols):
+        root = (c * group) % rows
+
+        @pl.when(row == root)
+        def _():
+            strip_own(c).start()
+            strip_start(c, strip_block(c))
+
     own_tile.wait()
     for copy in tile_copies:
         copy.wait()
@@ -105,32 +202,19 @@
     ]
     for copy in wide:
         copy.start()
-
-    def strip_block(c):
-        return panel.at[:, pl.ds((c * group // rows) * size, size)]
-
-    def strip_copy(c, d):
-        return remote(
-            strip_block(c), strip_in.at[c], strip_send.at[c, d], strip_recv.at[c], down(d)
-        )
+    for copy in late:
+        copy.start()
 
     for c in range(cols):
         root = (c * group) % rows
 
-        @pl.when(row == root)
+        @pl.when((row != root) & (lax.rem(row, 2) == root % 2))
         def _():
-            pltpu.make_async_copy(strip_block(c), strip_in.at[c], copy_sem.at[c]).start()
-            for d in range(1, rows):
-                strip_copy(c, d).start()
+            strip_sends(c, strip_in.at[c])[2][1].wait_recv()
+            strip_start(c, strip_in.at[c])
 
     for copy in wide:
         copy.wait()
-    panels = [
-        remote(panel, gathered.at[col], panel_send.at[d], panel_recv.at[d], across(d))
-        for d in range(1, cols)
-    ]
-    for copy in panels:
-        copy.start()
 
     for c in range(cols):
         for r in range(rows):
@@ -152,23 +236,26 @@
     own_strip = pltpu.make_async_copy(strip_in.at[col], strip_all.at[col], own_sem.at[2])
     for b in range(blocks):
         factor_block(work, upper, size, NB, b)
-        if b == blocks - 2:
+        if b == 0:
             for c in range(cols):
                 root = (c * group) % rows
 
                 @pl.when(row == root)
                 def _():
-                    pltpu.make_async_copy(strip_block(c), strip_in.at[c], copy_sem.at[c]).wait()
-                    for d in range(1, rows):
-                        strip_copy(c, d).wait_send()
-
-                @pl.when(row != root)
+                    strip_own(c).wait()
+
+                @pl.when(lax.rem(row, 2) != root % 2)
                 def _():
-                    strip_copy(c, 1).wait_recv()
+                    strip_sends(c, strip_in.at[c])[2][1].wait_recv()
 
             own_strip.start()
             for copy in exchange:
                 copy.start()
+            if relay:
+                for copy in (early[0], late[0], early[1], late[1]):
+                    copy.wait_recv()
+                for copy in forwards:
+                    copy.start()
     lower[...] = upper[...].T
     inverse[...] = work[:, size:]
     own_strip.wait()
@@ -180,8 +267,15 @@
         precision=HI,
         preferred_element_type=F32,
     )
+    for c in range(cols):
+        for cond, copy in strip_sends(c, strip_in.at[c]):
+            pl.when(cond)(copy.wait_send)
     own_panel.wait()
-    for copy in panels:
+    for copy in early + late:
+        copy.wait_send()
+    for copy in late[2:] if relay else late:
+        copy.wait_recv()
+    for copy in forwards:
         copy.wait()
 
 
@@ -197,32 +291,42 @@
 
 
 def update_kernel(
-    rows, cols, group, gathered, inverse, strip, lower, slab, diag_out, panel_out, slab_out
+    rows, cols, group, gathered, inverse, strip, lower, slab, diag_out, panel_out, slab_out,
+    inv_high, inv_low, strip_high, strip_low,
 ):
     row, col = lax.axis_index("prow"), lax.axis_index("pcol")
-    block, size = pl.program_id(0), slab.shape[0]
+    step, size = pl.program_id(0), strip.shape[0]
     high, low = diag_out.shape
-
-    full = gathered[...].reshape(size, size)
-    factor = dot_split(split(inverse[...]), split(full))
+    count = slab.shape[0] // size
+
+    @pl.when(step == 0)
+    def _():
+        inv_high[...], inv_low[...] = split(inverse[...])
+        strip_high[...], strip_low[...] = split(strip[...])
+
+    full = gathered[...].reshape(size, count * size)
+    factor = dot_split((inv_high[...], inv_low[...]), split(full))
     for c in range(cols):
 
         @pl.when(col == c)
         def _():
             panel_out[...] = factor[c * low : (c + 1) * low, :]
 
-            @pl.when(block == 0)
+            @pl.when(step == 0)
             def _():
                 start = pl.multiple_of(row * high, high)
                 diag_out[...] = lower[pl.ds(start, high), c * low : (c + 1) * low]
 
-    product = dot_split(split(factor.T), split(strip[...]))
-    shift = (block * rows + row - col * group) * size
-    keep = (
-        lax.broadcasted_iota(jnp.int32, slab.shape, 0) + shift
-        >= lax.broadcasted_iota(jnp.int32, slab.shape, 1)
-    )
-    slab_out[...] = jnp.where(keep, slab[...] - product, slab[...])
+    product = dot_split(split(factor.T), (strip_high[...], strip_low[...]))
+    for i in range(count):
+        here = slice(i * size, (i + 1) * size)
+        shift = ((step * count + i) * rows + row - col * group) * size
+        shape = (size, slab.shape[1])
+        keep = (
+            lax.broadcasted_iota(jnp.int32, shape, 0) + shift
+            >= lax.broadcasted_iota(jnp.int32, shape, 1)
+        )
+        slab_out[here, :] = jnp.where(keep, slab[here, :] - product[here, :], slab[here, :])
 
 
 def local(rows, cols, diag_block, panel, slab):
@@ -247,33 +351,35 @@
             pltpu.VMEM((cols, width, size), F32),
             pltpu.VMEM((cols, width, size), F32),
             dma((rows,)), dma((rows,)), dma((cols,)), dma((cols,)), dma((3,)),
-            dma((cols,)), dma((cols,)), dma((cols, rows)), dma((cols,)),
+            dma((cols, 4)), dma((cols, 4)), dma((cols, 3)), dma((cols,)),
             dma((cols,)), dma((cols,)), dma((cols,)),
         ],
         compiler_params=pltpu.CompilerParams(collective_id=0, has_side_effects=True),
         name="gather_factor",
     )(diag_block, panel.T)
+    tile = TILE if blocks % TILE == 0 else 1
     whole = pl.BlockSpec((size, size), lambda i: (0, 0))
     diag_out, panel_out, slab_out = pl.pallas_call(
         functools.partial(update_kernel, rows, cols, group),
-        grid=(blocks,),
+        grid=(blocks // tile,),
         out_shape=[
             jax.ShapeDtypeStruct(diag_block.shape, F32),
             jax.ShapeDtypeStruct((width, local_rows), F32),
             jax.ShapeDtypeStruct(slab.shape, F32),
         ],
         in_specs=[
-            pl.BlockSpec((cols, width, size), lambda i: (0, 0, i)),
+            pl.BlockSpec((cols, width, tile * size), lambda i: (0, 0, i)),
             whole,
             whole,
             whole,
-            pl.BlockSpec((size, slab.shape[1]), lambda i: (i, 0)),
+            pl.BlockSpec((tile * size, slab.shape[1]), lambda i: (i, 0)),
         ],
         out_specs=[
             pl.BlockSpec((high, low), lambda i: (0, 0)),
-            pl.BlockSpec((width, size), lambda i: (0, i)),
-            pl.BlockSpec((size, slab.shape[1]), lambda i: (i, 0)),
+            pl.BlockSpec((width, tile * size), lambda i: (0, i)),
+            pl.BlockSpec((tile * size, slab.shape[1]), lambda i: (i, 0)),
         ],
+        scratch_shapes=[pltpu.VMEM((size, size), jnp.bfloat16)] * 4,
         name="update",
     )(gathered, inverse, strip, lower, slab)
     return diag_out, panel_out.T, slab_out

time: 57.4 us -> 43.9 us (0.76)
  Pallas kernels: 56.5 us -> 43 us
    pallas_call x1, Pallas kernels: 47.1 us -> 36.4 us  [local(): pl.pallas_call(functools.partial(gather_kernel, rows, cols, group), out_s...]
    pallas_call x1, Pallas kernels: 9.36 us -> 6.66 us  [local(): pl.pallas_call(functools.partial(update_kernel, rows, cols, group), grid=...]
where the time goes in v3:
time: 43.9 us; the launch traced here: 43.7 us
  Pallas kernels  43 us (98%)
  between operations  0.64 us (1%)
    pallas_call x1, Pallas kernels, local(): pl.pallas_call(functools.partial(gather_kernel, rows, cols, group), out_s...  36.4 us
    pallas_call x1, Pallas kernels, local(): pl.pallas_call(functools.partial(update_kernel, rows, cols, group), grid=...  6.66 us

profile of v3, /device:TPU:0, one launch (start us, length us, event | category | flops | bytes accessed | tf_op | source)
XLA Modules:
  0.0 43.7 jit_solution(10556693720797929105)
XLA Ops:
  0.6 36.4 %gather_factor.1 = (f32[4,64,2048]{2,1,0:T(8,128)}, f32[256,256]{1,0:T(8,128)}, f32[256,256]{1,0:T(8,128)}, f32[256,256]{1,0:T(8,128)}) custom-call(f32[32,64]{1,0:T(8,128)} %diag.1, f32[64,2048]{1,0:T(8,128)} %bitcast.2), custom_call_target="tpu_custom_call" | custom-call | tf_op jit(solution)/shard_map/gather_factor/pallas_call | solution.py:342
  37.0 6.7 %update.1 = (f32[32,64]{1,0:T(8,128)}, f32[64,2048]{1,0:T(8,128)}, f32[2048,256]{1,0:T(8,128)}) custom-call(f32[4,64,2048]{2,1,0:T(8,128)} %get-tuple-element.10.gathered, f32[256,256]{1,0:T(8,128)} %get-tuple-element.11.inverse, f32[256,256]{1,0:T(8,128)} %get-tuple-element.12.strip, f32[256,256]{1,0:T(8,128)} %get-tuple-element.13.lower, f32[2048,256]{1,0:T(8,128)} %slab.1), custom_call_target="tpu_custom_call" | custom-call | tf_op jit(solution)/shard_map/update/pallas_call | solution.py:362

commit v4 on v3

--- a/solution.py
+++ b/solution.py
@@ -10,7 +10,7 @@
 HI = lax.Precision.HIGHEST
 F32 = jnp.float32
 NB = 64
-TILE = 2
+TILE = 4
 
 
 def small(groups, width):

time: 43.9 us -> 42.6 us (0.970)
  Pallas kernels: 43 us -> 41.7 us
    pallas_call x1, Pallas kernels: 6.66 us -> 5.32 us  [local(): pl.pallas_call(functools.partial(update_kernel, rows, cols, group), grid=...]
where the time goes in v4:
time: 42.6 us; the launch traced here: 42.3 us
  Pallas kernels  41.7 us (98%)
  between operations  0.64 us (2%)
    pallas_call x1, Pallas kernels, local(): pl.pallas_call(functools.partial(gather_kernel, rows, cols, group), out_s...  36.4 us
    pallas_call x1, Pallas kernels, local(): pl.pallas_call(functools.partial(update_kernel, rows, cols, group), grid=...  5.32 us

profile of v4, /device:TPU:0, one launch (start us, length us, event | category | flops | bytes accessed | tf_op | source)
XLA Modules:
  0.0 42.3 jit_solution(16227313379652588945)
XLA Ops:
  0.6 36.4 %gather_factor.1 = (f32[4,64,2048]{2,1,0:T(8,128)}, f32[256,256]{1,0:T(8,128)}, f32[256,256]{1,0:T(8,128)}, f32[256,256]{1,0:T(8,128)}) custom-call(f32[32,64]{1,0:T(8,128)} %diag.1, f32[64,2048]{1,0:T(8,128)} %bitcast.2), custom_call_target="tpu_custom_call" | custom-call | tf_op jit(solution)/shard_map/gather_factor/pallas_call | solution.py:342
  37.0 5.3 %update.1 = (f32[32,64]{1,0:T(8,128)}, f32[64,2048]{1,0:T(8,128)}, f32[2048,256]{1,0:T(8,128)}) custom-call(f32[4,64,2048]{2,1,0:T(8,128)} %get-tuple-element.10.gathered, f32[256,256]{1,0:T(8,128)} %get-tuple-element.11.inverse, f32[256,256]{1,0:T(8,128)} %get-tuple-element.12.strip, f32[256,256]{1,0:T(8,128)} %get-tuple-element.13.lower, f32[2048,256]{1,0:T(8,128)} %slab.1), custom_call_target="tpu_custom_call" | custom-call | tf_op jit(solution)/shard_map/update/pallas_call | solution.py:362

commit v5 on v4

--- a/solution.py
+++ b/solution.py
@@ -87,7 +87,7 @@
     rows, cols, group,
     diag, panel,
     gathered, lower, inverse, strip,
-    tiles, work, upper, strip_in, strip_all,
+    tiles, work, upper, strip_all,
     tile_send, tile_recv, wide_send, wide_recv, own_sem,
     panel_send, panel_recv, strip_send, strip_recv, ex_send, ex_recv, copy_sem,
 ):
@@ -152,46 +152,61 @@
     else:
         early = []
         late = [piece_copy(i, d, across(d)) for d in range(1, cols) for i in range(4)]
-    for copy in early:
-        copy.start()
+    my_root = lax.rem(col * group, rows)
+    place, origin, last = row // 2, my_root // 2, rows // 2 - 1
+    spine = lax.rem(row, 2) == lax.rem(my_root, 2)
+    steps = [
+        (spine & (place >= origin) & (place < last), 2),
+        (spine & (place <= origin) & (place > 0), -2),
+        (spine, 1 - 2 * lax.rem(my_root, 2)),
+    ]
 
     def strip_block(c):
-        return panel.at[:, pl.ds((c * group // rows) * size, size)]
-
-    def strip_sends(c, src):
-        root = (c * group) % rows
-        place, origin, last = row // 2, root // 2, rows // 2 - 1
-        spine = lax.rem(row, 2) == root % 2
-        steps = [
-            (spine & (place >= origin) & (place < last), 2),
-            (spine & (place <= origin) & (place > 0), -2),
-            (spine, 1 - 2 * (root % 2)),
-        ]
+        start = pl.multiple_of(c * group // rows * size, size)
+        return panel.at[:, pl.ds(start, size)]
+
+    def strip_give(c):
+        give = (row == (c * group) % rows) & (col != c)
+        return give, remote(
+            strip_block(c), strip_all.at[col], ex_send.at[c], ex_recv.at[col], {"pcol": c}
+        )
+
+    def strip_take(c):
+        return remote(
+            strip_block(c), strip_all.at[c], ex_send.at[c], ex_recv.at[c], {"pcol": lax.rem(col + 1, cols)}
+        )
+
+    def strip_sends(c):
+        view = strip_all.at[c]
         return [
             (
                 cond,
                 remote(
-                    src, strip_in.at[c], strip_send.at[c, i], strip_recv.at[c],
+                    view, view, strip_send.at[c, i], strip_recv.at[c],
                     {"prow": lax.rem(row + step + rows, rows)},
                 ),
             )
             for i, (cond, step) in enumerate(steps)
         ]
 
-    def strip_start(c, src):
-        for cond, copy in strip_sends(c, src):
+    def strip_start(c):
+        for cond, copy in strip_sends(c):
             pl.when(cond)(copy.start)
 
-    def strip_own(c):
-        return pltpu.make_async_copy(strip_block(c), strip_in.at[c], copy_sem.at[c])
-
     for c in range(cols):
-        root = (c * group) % rows
-
-        @pl.when(row == root)
-        def _():
-            strip_own(c).start()
-            strip_start(c, strip_block(c))
+        give, copy = strip_give(c)
+        pl.when(give)(copy.start)
+    for copy in early:
+        copy.start()
+
+    @pl.when(row == my_root)
+    def _():
+        own = pltpu.make_async_copy(strip_block(col), strip_all.at[col], copy_sem.at[0])
+        own.start()
+        own.wait()
+        for c in range(cols):
+            pl.when(col != c)(strip_take(c).wait_recv)
+            strip_start(c)
 
     own_tile.wait()
     for copy in tile_copies:
@@ -205,13 +220,11 @@
     for copy in late:
         copy.start()
 
-    for c in range(cols):
-        root = (c * group) % rows
-
-        @pl.when((row != root) & (lax.rem(row, 2) == root % 2))
-        def _():
-            strip_sends(c, strip_in.at[c])[2][1].wait_recv()
-            strip_start(c, strip_in.at[c])
+    @pl.when((row != my_root) & spine)
+    def _():
+        for c in range(cols):
+            strip_sends(c)[2][1].wait_recv()
+            strip_start(c)
 
     for copy in wide:
         copy.wait()
@@ -226,31 +239,9 @@
     ).astype(F32)
 
     blocks = size // NB
-    exchange = [
-        remote(
-            strip_in.at[lax.rem(col + d, cols)], strip_all.at[col],
-            ex_send.at[d], ex_recv.at[d], across(d),
-        )
-        for d in range(1, cols)
-    ]
-    own_strip = pltpu.make_async_copy(strip_in.at[col], strip_all.at[col], own_sem.at[2])
     for b in range(blocks):
         factor_block(work, upper, size, NB, b)
         if b == 0:
-            for c in range(cols):
-                root = (c * group) % rows
-
-                @pl.when(row == root)
-                def _():
-                    strip_own(c).wait()
-
-                @pl.when(lax.rem(row, 2) != root % 2)
-                def _():
-                    strip_sends(c, strip_in.at[c])[2][1].wait_recv()
-
-            own_strip.start()
-            for copy in exchange:
-                copy.start()
             if relay:
                 for copy in (early[0], late[0], early[1], late[1]):
                     copy.wait_recv()
@@ -258,9 +249,12 @@
                     copy.start()
     lower[...] = upper[...].T
     inverse[...] = work[:, size:]
-    own_strip.wait()
-    for copy in exchange:
-        copy.wait()
+
+    @pl.when(lax.rem(row, 2) != lax.rem(my_root, 2))
+    def _():
+        for c in range(cols):
+            strip_sends(c)[2][1].wait_recv()
+
     strip[...] = jnp.dot(
         work[:, size:],
         strip_all[...].reshape(size, size),
@@ -268,7 +262,9 @@
         preferred_element_type=F32,
     )
     for c in range(cols):
-        for cond, copy in strip_sends(c, strip_in.at[c]):
+        give, copy = strip_give(c)
+        pl.when(give)(copy.wait_send)
+        for cond, copy in strip_sends(c):
             pl.when(cond)(copy.wait_send)
     own_panel.wait()
     for copy in early + late:
@@ -348,7 +344,6 @@
             pltpu.VMEM((cols, rows, high, low), F32),
             pltpu.VMEM((size, 2 * size), F32),
             pltpu.VMEM((size, size), F32),
-            pltpu.VMEM((cols, width, size), F32),
             pltpu.VMEM((cols, width, size), F32),
             dma((rows,)), dma((rows,)), dma((cols,)), dma((cols,)), dma((3,)),
             dma((cols, 4)), dma((cols, 4)), dma((cols, 3)), dma((cols,)),

time: 42.6 us -> 41 us (0.962)
  Pallas kernels: 41.7 us -> 40.1 us
    pallas_call x1, Pallas kernels: 36.4 us -> 34.8 us  [local(): pl.pallas_call(functools.partial(gather_kernel, rows, cols, group), out_s...]
where the time goes in v5:
time: 41 us; the launch traced here: 40.7 us
  Pallas kernels  40.1 us (98%)
  between operations  0.64 us (2%)
    pallas_call x1, Pallas kernels, local(): pl.pallas_call(functools.partial(gather_kernel, rows, cols, group), out_s...  34.8 us
    pallas_call x1, Pallas kernels, local(): pl.pallas_call(functools.partial(update_kernel, rows, cols, group), grid=...  5.33 us

profile of v5, /device:TPU:0, one launch (start us, length us, event | category | flops | bytes accessed | tf_op | source)
XLA Modules:
  0.0 40.7 jit_solution(16922085586052482937)
XLA Ops:
  0.6 34.8 %gather_factor.1 = (f32[4,64,2048]{2,1,0:T(8,128)}, f32[256,256]{1,0:T(8,128)}, f32[256,256]{1,0:T(8,128)}, f32[256,256]{1,0:T(8,128)}) custom-call(f32[32,64]{1,0:T(8,128)} %diag.1, f32[64,2048]{1,0:T(8,128)} %bitcast.2), custom_call_target="tpu_custom_call" | custom-call | tf_op jit(solution)/shard_map/gather_factor/pallas_call | solution.py:338
  35.4 5.3 %update.1 = (f32[32,64]{1,0:T(8,128)}, f32[64,2048]{1,0:T(8,128)}, f32[2048,256]{1,0:T(8,128)}) custom-call(f32[4,64,2048]{2,1,0:T(8,128)} %get-tuple-element.10.gathered, f32[256,256]{1,0:T(8,128)} %get-tuple-element.11.inverse, f32[256,256]{1,0:T(8,128)} %get-tuple-element.12.strip, f32[256,256]{1,0:T(8,128)} %get-tuple-element.13.lower, f32[2048,256]{1,0:T(8,128)} %slab.1), custom_call_target="tpu_custom_call" | custom-call | tf_op jit(solution)/shard_map/update/pallas_call | solution.py:357
